TPU v7x, 32 devices: a whole 2x2x4 slice. The times are simulated.
32 devices in a mesh: row: 8 (over y, x, core), col: 4 (over z).
Axes of the slice: x: 2, y: 2, z: 4, core: 2. Of those that a mesh axis runs over, the one named last changes fastest.
Arguments:
- skew_matrix: float32 [16384, 16384], P('row', 'col'), may hold values from -80 to 80, as said below
- first_reflector: float32 [16384, 128], P('row'), may hold values from -0.05625 to 0.05625
- first_factor: float32 [128, 128], replicated, may hold values from -0.6 to 1.5, as said below
- second_reflector: float32 [16384, 128], P('row'), may hold values from -0.05625 to 0.05625
- second_factor: float32 [128, 128], replicated, may hold values from -0.6 to 1.5, as said below
- vectors: float32 [16384, 4096], P('row', 'col'), may hold values from -6 to 6
Outputs:
- updated_matrix: float32 [16384, 16384], P('row', 'col')
- back_vectors: float32 [16384, 4096], P('row', 'col')
Inputs may be any that keep to these rules, and one draw needn't show every extreme that they name: skew_matrix is skew-symmetric: entry (i, j) equals minus entry (j, i) exactly. first_factor is upper triangular with a positive diagonal. second_factor is upper triangular with a positive diagonal.
All inputs are finite; a program needn't handle non-finite values.
Results may differ from a plain program's by a relative error of at most 0.000059.
Values sent between devices are 32-bit elements; how exact they have to be, the bound alone decides.
A program may use at most 192 MiB of HBM per device.

v0:
```python
import jax
import jax.numpy as jnp
from jax import lax
from jax.sharding import PartitionSpec as P


def multiply(left, right):
    return jnp.dot(left, right, precision=lax.Precision.HIGHEST, preferred_element_type=jnp.float32)


def inner_rows(left, right):
    return lax.dot_general(
        left,
        right,
        (((0,), (0,)), ((), ())),
        precision=lax.Precision.HIGHEST,
        preferred_element_type=jnp.float32,
    )


def transform(matrix, own_rows, col_rows, factor):
    partial_rows = multiply(matrix, col_rows)
    summed_rows = lax.psum(partial_rows, "col")
    partial_cols = inner_rows(matrix, own_rows)
    summed_cols = lax.psum(partial_cols, "row")
    plain_cols = -summed_cols
    gram = lax.psum(inner_rows(own_rows, summed_rows), "row")
    correction = multiply(multiply(factor.T, gram), factor)
    fixed_rows = multiply(summed_rows, factor) - 0.5 * multiply(own_rows, correction)
    fixed_cols = multiply(plain_cols, factor) - 0.5 * multiply(col_rows, correction)
    left = jnp.concatenate([own_rows, -fixed_rows], axis=1)
    right = jnp.concatenate([fixed_cols, col_rows], axis=1)
    update = lax.dot_general(
        left,
        right,
        (((1,), (1,)), ((), ())),
        precision=lax.Precision.HIGHEST,
        preferred_element_type=jnp.float32,
    )
    return matrix + update


def shards(skew_matrix, first_reflector, first_factor, second_reflector, second_factor, vectors):
    joined = jnp.concatenate([first_reflector, second_reflector], axis=1)
    correlation, projected = lax.psum(
        (inner_rows(first_reflector, second_reflector), inner_rows(joined, vectors)), "row"
    )
    top_right = -multiply(multiply(first_factor, correlation), second_factor)
    zeros_block = jnp.zeros_like(second_factor)
    compact = jnp.concatenate(
        [
            jnp.concatenate([first_factor, top_right], axis=1),
            jnp.concatenate([zeros_block, second_factor], axis=1),
        ],
        axis=0,
    )
    back_vectors = vectors - multiply(joined, multiply(compact, projected))
    cols_here = skew_matrix.shape[1]
    col_index = lax.axis_index("col")
    whole_first, whole_second = (
        lax.all_gather(first_reflector, "row", axis=0, tiled=True),
        lax.all_gather(second_reflector, "row", axis=0, tiled=True),
    )
    col_start = col_index * cols_here
    panel_first = lax.dynamic_slice_in_dim(whole_first, col_start, cols_here, 0)
    panel_second = lax.dynamic_slice_in_dim(whole_second, col_start, cols_here, 0)
    inner = transform(skew_matrix, first_reflector, panel_first, first_factor)
    updated_matrix = transform(inner, second_reflector, panel_second, second_factor)
    return (updated_matrix, back_vectors)


def solution(mesh):
    in_specs = (P("row", "col"), P("row", None), P(), P("row", None), P(), P("row", "col"))
    out_specs = (P("row", "col"), P("row", "col"))
    return jax.shard_map(shards, mesh=mesh, in_specs=in_specs, out_specs=out_specs, check_vma=False)
```

profile of v0, /device:TPU:0, one launch (start us, length us, event | category | flops | bytes accessed | tf_op | source)
XLA Modules:
  0.0 549.0 jit_solution(17140156105039725318)
XLA Ops:
  7.2 0.0 all-gather.3.cloned.1.call-start
  7.2 0.7 all-gather.3.cloned.1.call-update
  7.9 0.0 all-reduce.8.cloned.1.call-start
  7.9 58.9 %all-gather.3.cloned.1.call-done = f32[16384,128]{1,0:T(8,128)} async-done(((f32[2048,128]{1,0:T(8,128)}), f32[16384,128]{1,0:T(8,128)}) %all-gather.3.cloned.1.call-update) | async-done | bytes 8388624 | tf_op jit(solution)/shard_map/all_gather | solution.py:61
  66.9 1.7 constant_dynamic-slice_fusion.1
  68.6 0.0 copy-start.4
  68.6 1.3 copy-done.4
  69.9 41.9 %convolution_bitcast_fusion = f32[2048,128]{0,1:T(8,128)} fusion(f32[4096,128]{1,0:T(8,128)S(1)} %constant_dynamic-slice_fusion.1, f32[2048,4096]{1,0:T(8,128)} %param.6), kind=kOutput, calls=%fused_computation.13 | convolution fusion | flops 12884901888 | bytes 36700160 | tf_op jit(solution)/shard_map/dot_general | solution.py:8
  111.8 0.0 copy-start
  111.8 0.0 copy-start.1
  111.8 0.0 all-reduce.8.cloned.1.call-update
  111.8 0.0 all-gather.5.cloned.1.call-start
  111.9 0.7 all-gather.5.cloned.1.call-update
  112.6 0.0 all-reduce.14.cloned.1.call-start
  112.6 0.4 copy-done
  113.0 1.1 constant_dynamic-update-slice_fusion.1
  114.1 0.0 copy-done.1
  114.1 1.1 constant_dynamic-update-slice_fusion
  115.2 57.1 %fusion.39 = f32[4096,128]{1,0:T(8,128)} fusion(f32[2048,4096]{1,0:T(8,128)} %param.6, f32[2048,128]{1,0:T(8,128)S(1)} %copy-done), kind=kOutput, calls=%fused_computation.56 | convolution fusion | flops 12884901888 | bytes 36700160 | tf_op jit(solution)/shard_map/dot_general | solution.py:12
  172.3 0.0 all-reduce.8.cloned.1.call-done
  172.3 3.1 convolution_bitcast_fusion.2
  175.4 0.0 all-reduce.14.cloned.1.call-update
  175.4 0.0 all-reduce.10.cloned.1.call-start
  175.5 11.1 %fusion.47 = f32[256,1024]{1,0:T(8,128)} fusion(f32[2048,256]{1,0:T(8,128)} %constant_dynamic-update-slice_fusion, f32[2048,1024]{1,0:T(8,128)} %param.11), kind=kOutput, calls=%fused_computation.64 | convolution fusion | flops 6442450944 | bytes 11534336 | tf_op jit(solution)/shard_map/dot_general | solution.py:12
  186.5 2.4 fusion.45
  189.0 30.4 %all-gather.5.cloned.1.call-done = f32[16384,128]{1,0:T(8,128)} async-done(((f32[2048,128]{1,0:T(8,128)}), f32[16384,128]{1,0:T(8,128)}) %all-gather.5.cloned.1.call-update) | async-done | bytes 8388624 | tf_op jit(solution)/shard_map/all_gather | solution.py:62
  219.3 3.2 constant_dynamic-slice_fusion
  222.6 0.0 copy-done.8
  222.6 0.0 copy-done.6
  222.6 1.8 fusion.36
  224.4 60.9 %all-reduce.14.cloned.1.call-done = (f32[4096,128]{1,0:T(8,128)}, f32[128,128]{0,1:T(8,128)}) async-done(((f32[4096,128]{1,0:T(8,128)}, f32[128,128]{0,1:T(8,128)}), (f32[4096,128]{1,0:T(8,128)}, f32[128,128]{0,1:T(8,128)})) %all-reduce.14.cloned.1.call-update) | async-done | bytes 2162704 | tf_op jit(solution)/shard_map/psum | solution.py:25
  285.3 3.6 fusion.22
  288.9 0.0 copy-done.12
  288.9 0.2 fusion.37
  289.1 0.3 fusion.38
  289.4 0.0 copy-done.5
  289.4 1.9 fusion.1
  291.3 1.0 fusion.13
  292.3 0.0 copy-start.2
  292.3 33.7 %convolution_add_fusion.1 = f32[2048,4096]{1,0:T(8,128)} fusion(f32[2048,4096]{1,0:T(8,128)} %param.6, f32[4096,128]{1,0:T(8,128)S(1)} %copy-done.5, f32[4096,128]{1,0:T(8,128)S(1)} %fusion.1, f32[2048,128]{1,0:T(8,128)S(1)} %fusion.13, f32[2048,128]{1,0:T(8,128)S(1)} %copy-done), kind=kOutput, calls=%fused_computation.1 | convolution fusion | flops 25779765248 | bytes 73400320 | tf_op jit(solution)/shard_map/dot_general | solution.py:33
  325.9 0.0 copy-done.2
  325.9 30.9 %fusion.40 = f32[2048,128]{1,0:T(8,128)} fusion(f32[2048,4096]{1,0:T(8,128)} %convolution_add_fusion.1, f32[4096,128]{1,0:T(8,128)S(1)} %copy-done.2), kind=kOutput, calls=%fused_computation.57 | convolution fusion | flops 12884901888 | bytes 36700160 | tf_op jit(solution)/shard_map/dot_general | solution.py:8
  356.8 0.0 all-reduce.10.cloned.1.call-update
  356.8 0.0 all-reduce.12.cloned.1.call-start
  356.9 57.1 %fusion.44 = f32[4096,128]{1,0:T(8,128)} fusion(f32[2048,4096]{1,0:T(8,128)} %convolution_add_fusion.1, f32[2048,128]{1,0:T(8,128)S(1)} %copy-done.1), kind=kOutput, calls=%fused_computation.61 | convolution fusion | flops 12884901888 | bytes 36700160 | tf_op jit(solution)/shard_map/dot_general | solution.py:12
  414.0 0.0 all-reduce.10.cloned.1.call-done
  414.0 3.7 convolution_bitcast_fusion.1
  417.7 0.0 all-reduce.12.cloned.1.call-update
  417.7 1.2 copy-done.7
  418.9 0.0 copy-done.9
  418.9 1.0 fusion.41
  419.9 68.0 %all-reduce.12.cloned.1.call-done = (f32[4096,128]{1,0:T(8,128)}, f32[128,128]{0,1:T(8,128)}, f32[256,1024]{1,0:T(8,128)}, f32[128,128]{1,0:T(8,128)}) async-done(((f32[4096,128]{1,0:T(8,128)}, f32[128,128]{0,1:T(8,128)}, f32[256,1024]{1,0:T(8,128)}, f32[128,128]{1,0:T(8,128)}), (f32[4096,128]{1,0:T(8,128)}, f32[128,128]{0,1:T(8,128)}, f32[256,1024]{1,0:T(8,128)}, ...) | async-done | bytes 3276816 | tf_op jit(solution)/shard_map/psum | solution.py:25
  487.9 3.6 fusion.20
  491.4 0.0 copy-done.13
  491.5 0.2 fusion.42
  491.7 0.3 fusion.43
  492.0 0.0 copy-done.3
  492.0 1.9 fusion
  493.9 1.0 fusion.10
  494.9 0.3 fusion.46
  495.2 0.3 convolution_negate_fusion
  495.5 1.0 fusion.24
  496.5 12.2 %convolution_subtract_fusion = f32[2048,1024]{1,0:T(8,128)} fusion(f32[2048,1024]{1,0:T(8,128)} %param.11, f32[2048,256]{1,0:T(8,128)} %constant_dynamic-update-slice_fusion, f32[256,1024]{1,0:T(8,128)S(1)} %fusion.24), kind=kOutput, calls=%fused_computation.6 | convolution fusion | flops 6444548096 | bytes 19922944 | tf_op jit(solution)/shard_map/dot_general | solution.py:8
  508.7 33.0 %convolution_add_fusion = f32[2048,4096]{1,0:T(8,128)} fusion(f32[2048,4096]{1,0:T(8,128)} %convolution_add_fusion.1, f32[4096,128]{1,0:T(8,128)S(1)} %copy-done.3, f32[4096,128]{1,0:T(8,128)S(1)} %fusion, f32[2048,128]{1,0:T(8,128)S(1)} %fusion.10, f32[2048,128]{1,0:T(8,128)S(1)} %copy-done.1), kind=kOutput, calls=%fused_computation | convolution fusion | flops 25779765248 | bytes 73400320 | tf_op jit(solution)/shard_map/dot_general | solution.py:33
  (12 shorter events, 0.0 us)
Async XLA Ops:
  7.2 59.7 %all-gather.3.cloned.1.call-start = ((), (), s32[]{:S(2)}) async-start(), calls=%async_computation | async-start | bytes 9437184 | tf_op jit(solution)/shard_map/all_gather | solution.py:61
  7.9 164.4 %all-reduce.8.cloned.1.call-start = ((), (), s32[]{:S(2)}) async-start(), calls=%async_computation.1 | async-start | bytes 2097152 | tf_op jit(solution)/shard_map/psum | solution.py:23
  68.6 1.3 copy-start.4
  111.8 1.2 copy-start
  111.8 2.3 copy-start.1
  111.8 107.5 %all-gather.5.cloned.1.call-start = ((), (), s32[]{:S(2)}) async-start(), calls=%async_computation.2 | async-start | bytes 9437184 | tf_op jit(solution)/shard_map/all_gather | solution.py:62
  112.6 172.7 %all-reduce.14.cloned.1.call-start = ((), (), s32[]{:S(2)}) async-start(), calls=%async_computation.5 | async-start | bytes 4325376 | tf_op jit(solution)/shard_map/psum | solution.py:25
  175.4 238.6 %all-reduce.10.cloned.1.call-start = ((), (), s32[]{:S(2)}) async-start(), calls=%async_computation.3 | async-start | bytes 2097152 | tf_op jit(solution)/shard_map/psum | solution.py:23
  189.0 33.6 %copy-start.8 = (f32[128,128]{1,0:T(8,128)S(1)}, f32[128,128]{1,0:T(8,128)}, u32[]{:S(2)}) copy-start(f32[128,128]{1,0:T(8,128)} %param.8) | copy-start | bytes 196612
  219.3 3.2 copy-start.6
  285.3 3.6 copy-start.12
  285.3 4.1 copy-start.5
  292.3 33.7 %copy-start.2 = (f32[4096,128]{1,0:T(8,128)S(1)}, f32[4096,128]{1,0:T(8,128)}, u32[]{:S(2)}) copy-start(f32[4096,128]{1,0:T(8,128)} %constant_dynamic-slice_fusion) | copy-start | bytes 6291460
  356.8 131.0 %all-reduce.12.cloned.1.call-start = ((), (), s32[]{:S(2)}) async-start(), calls=%async_computation.4 | async-start | bytes 6553600 | tf_op jit(solution)/shard_map/psum | solution.py:25
  417.7 1.2 copy-start.7
  417.7 1.2 copy-start.9
  487.9 3.6 copy-start.13
  487.9 4.1 copy-start.3
  493.8 1.0 copy-start.11
  493.9 1.6 copy-start.10
Sparse Core Ops, SparseCore 0:
  9.9 56.9 all-gather.2
  112.0 51.8 all-reduce.7
  165.8 53.5 all-gather.4
  223.1 62.1 all-reduce.13
  357.0 51.0 all-reduce.9
  417.8 70.0 all-reduce.11
where the time goes:
time: 559 us; the launch traced here: 549 us
  matrix products  304 us (54%)
  waiting for transfers between devices  220 us (39%)
  between operations  14.8 us (3%)
  local copies, waits for them, and re-layouts  10 us (2%)
    dot_general x6, matrix products, inner_rows(): lax.dot_general(left, right, (((0,), (0,)), ((), ())), precision=lax.Prec...  134 us
    psum x2, waiting for transfers between devices, transform(): summed_cols = lax.psum(partial_cols, 'row')  129 us
    dot_general x18, matrix products, multiply(): jnp.dot(left, right, precision=lax.Precision.HIGHEST, preferred_element_t...  103 us
    dot_general x2, matrix products, transform(): lax.dot_general(left, right, (((1,), (1,)), ((), ())), precision=lax.Prec...  66.7 us
    all_gather x1, waiting for transfers between devices, shards(): lax.all_gather(first_reflector, 'row', axis=0, tiled=True)  58.9 us
    all_gather x1, waiting for transfers between devices, shards(): lax.all_gather(second_reflector, 'row', axis=0, tiled=True)  30.4 us
  transfers between devices with their start and end apart: 6, of which 4 were waited for; matrix products, arithmetic and copies ran while one was open for 25% of the time, Pallas kernels for 0%

commit v1 on v0

--- a/solution.py
+++ b/solution.py
@@ -22,7 +22,7 @@
     partial_rows = multiply(matrix, col_rows)
     summed_rows = lax.psum(partial_rows, "col")
     partial_cols = inner_rows(matrix, own_rows)
-    summed_cols = lax.psum(partial_cols, "row")
+    summed_cols = jnp.sum(lax.all_gather(partial_cols, "row"), axis=0)
     plain_cols = -summed_cols
     gram = lax.psum(inner_rows(own_rows, summed_rows), "row")
     correction = multiply(multiply(factor.T, gram), factor)

time: 559 us -> 712 us (1.27)
  waiting for transfers between devices: 220 us -> 351 us
  other arithmetic: 0 us -> 16.3 us
    all_gather x0 -> x2, waiting for transfers between devices: none -> 157 us  [transform(): summed_cols = jnp.sum(lax.all_gather(partial_cols, 'row'), axis=0)]
    psum x2, waiting for transfers between devices: 0.04 us -> 88.8 us  [transform(): summed_rows = lax.psum(partial_rows, 'col')]
    psum x2, waiting for transfers between devices: 129 us -> 44.5 us  [transform(): gram = lax.psum(inner_rows(own_rows, summed_rows), 'row')]
    all_gather x1, waiting for transfers between devices: 30.4 us -> 0.01 us  [shards(): lax.all_gather(second_reflector, 'row', axis=0, tiled=True)]
    reduce_sum x0 -> x2, other arithmetic: none -> 16.3 us  [transform(): summed_cols = jnp.sum(lax.all_gather(partial_cols, 'row'), axis=0)]
  transfers between devices with their start and end apart: 6 -> 8, of which waited for: 4 -> 6; matrix products, arithmetic and copies ran while one was open for 25% -> 23% of each run, Pallas kernels for 0% -> 0%
where the time goes in v1:
time: 712 us; the launch traced here: 701 us
  waiting for transfers between devices  351 us (49%)
  matrix products  309 us (43%)
  other arithmetic  16.3 us (2%)
  between operations  14.8 us (2%)
  local copies, waits for them, and re-layouts  9.27 us (1%)
    all_gather x2, waiting for transfers between devices, transform(): summed_cols = jnp.sum(lax.all_gather(partial_cols, 'row'), axis=0)  157 us
    dot_general x6, matrix products, inner_rows(): lax.dot_general(left, right, (((0,), (0,)), ((), ())), precision=lax.Prec...  134 us
    dot_general x18, matrix products, multiply(): jnp.dot(left, right, precision=lax.Precision.HIGHEST, preferred_element_t...  109 us
    psum x2, waiting for transfers between devices, transform(): summed_rows = lax.psum(partial_rows, 'col')  88.8 us
    dot_general x2, matrix products, transform(): lax.dot_general(left, right, (((1,), (1,)), ((), ())), precision=lax.Prec...  66.7 us
    all_gather x1, waiting for transfers between devices, shards(): lax.all_gather(first_reflector, 'row', axis=0, tiled=True)  58.9 us
    psum x2, waiting for transfers between devices, transform(): gram = lax.psum(inner_rows(own_rows, summed_rows), 'row')  44.5 us
    reduce_sum x2, other arithmetic, transform(): summed_cols = jnp.sum(lax.all_gather(partial_cols, 'row'), axis=0)  16.3 us
  transfers between devices with their start and end apart: 8, of which 6 were waited for; matrix products, arithmetic and copies ran while one was open for 23% of the time, Pallas kernels for 0%

profile of v1, /device:TPU:0, one launch (start us, length us, event | category | flops | bytes accessed | tf_op | source)
XLA Modules:
  0.0 701.4 jit_solution(14762369002562291343)
XLA Ops:
  7.2 0.0 all-gather.7.cloned.1.call-start
  7.2 0.7 all-gather.7.cloned.1.call-update
  7.9 0.0 all-reduce.7.cloned.1.call-start
  7.9 58.9 %all-gather.7.cloned.1.call-done = f32[16384,128]{1,0:T(8,128)} async-done(((f32[2048,128]{1,0:T(8,128)}), f32[16384,128]{1,0:T(8,128)}) %all-gather.7.cloned.1.call-update) | async-done | bytes 8388624 | tf_op jit(solution)/shard_map/all_gather | solution.py:61
  66.9 1.7 constant_dynamic-slice_fusion.1
  68.6 41.8 %convolution_bitcast_fusion = f32[2048,128]{0,1:T(8,128)} fusion(f32[4096,128]{1,0:T(8,128)S(1)} %constant_dynamic-slice_fusion.1, f32[2048,4096]{1,0:T(8,128)} %param.6), kind=kOutput, calls=%fused_computation.13 | convolution fusion | flops 12884901888 | bytes 36700160 | tf_op jit(solution)/shard_map/dot_general | solution.py:8
  110.4 0.0 copy-start
  110.4 0.0 all-reduce.7.cloned.1.call-update
  110.4 0.0 all-gather.9.cloned.1.call-start
  110.5 0.7 all-gather.9.cloned.1.call-update
  111.2 0.0 all-reduce.9.cloned.1.call-start
  111.2 51.3 %all-reduce.7.cloned.1.call-done = f32[2048,128]{0,1:T(8,128)} async-done(((f32[2048,128]{0,1:T(8,128)}), f32[2048,128]{0,1:T(8,128)}) %all-reduce.7.cloned.1.call-update) | async-done | bytes 1048592 | tf_op jit(solution)/shard_map/psum | solution.py:23
  162.5 0.0 copy-done
  162.5 3.0 convolution_bitcast_fusion.2
  165.5 0.0 all-reduce.9.cloned.1.call-update
  165.5 0.0 all-gather.11.cloned.1.call-start
  165.5 56.9 %fusion.39 = f32[4096,128]{1,0:T(8,128)} fusion(f32[2048,4096]{1,0:T(8,128)} %param.6, f32[2048,128]{1,0:T(8,128)S(1)} %copy-done), kind=kOutput, calls=%fused_computation.56 | convolution fusion | flops 12884901888 | bytes 36700160 | tf_op jit(solution)/shard_map/dot_general | solution.py:12
  222.4 0.0 all-gather.11.cloned.1.call-update
  222.4 0.0 all-reduce.11.cloned.1.call-start
  222.5 1.1 constant_dynamic-update-slice_fusion.1
  223.6 3.2 constant_dynamic-slice_fusion
  226.8 0.0 copy-done.9
  226.8 0.0 copy-done.7
  226.8 2.8 fusion.36
  229.6 44.5 %all-reduce.9.cloned.1.call-done = f32[128,128]{0,1:T(8,128)} async-done(((f32[128,128]{0,1:T(8,128)}), f32[128,128]{0,1:T(8,128)}) %all-reduce.9.cloned.1.call-update) | async-done | bytes 65552 | tf_op jit(solution)/shard_map/psum | solution.py:27
  274.1 1.0 fusion.37
  275.1 0.3 fusion.38
  275.4 3.2 fusion.13
  278.6 87.0 %all-gather.11.cloned.1.call-done = f32[32768,128]{1,0:T(8,128)} async-done(((f32[4096,128]{1,0:T(8,128)}), f32[32768,128]{1,0:T(8,128)}) %all-gather.11.cloned.1.call-update) | async-done | bytes 16777232 | tf_op jit(solution)/shard_map/all_gather | solution.py:25
  365.5 8.1 %reduce_sum.18 = f32[4096,128]{1,0:T(8,128)} reduce(f32[8,4096,128]{2,1,0:T(8,128)} %bitcast.66, f32[]{:T(128)} %constant.3.clone.1), dimensions={0}, to_apply=%region_2.0 | reduce | flops 3670016 | bytes 18874372 | tf_op jit(solution)/shard_map/reduce_sum | solution.py:25
  373.7 3.4 fusion.22
  377.1 0.0 copy-start.6
  377.1 1.9 fusion.1
  379.0 0.0 copy-done.6
  379.0 33.4 %convolution_add_fusion.1 = f32[2048,4096]{1,0:T(8,128)} fusion(f32[2048,4096]{1,0:T(8,128)} %param.6, f32[4096,128]{1,0:T(8,128)S(1)} %constant_dynamic-slice_fusion.1, f32[4096,128]{1,0:T(8,128)S(1)} %fusion.1, f32[2048,128]{1,0:T(8,128)S(1)} %copy-done.6, f32[2048,128]{1,0:T(8,128)S(1)} %copy-done), kind=kOutput, calls=%fused_computation.1 | convolution fusion | flops 25779765248 | bytes 73400320 | tf_op jit(solution)/shard_map/dot_general | solution.py:33
  412.4 31.0 %fusion.40 = f32[2048,128]{1,0:T(8,128)} fusion(f32[2048,4096]{1,0:T(8,128)} %convolution_add_fusion.1, f32[4096,128]{1,0:T(8,128)S(1)} %copy-done.2), kind=kOutput, calls=%fused_computation.57 | convolution fusion | flops 12884901888 | bytes 36700160 | tf_op jit(solution)/shard_map/dot_general | solution.py:8
  443.4 0.0 all-reduce.11.cloned.1.call-update
  443.4 0.4 all-reduce.13.cloned.1.call-start
  443.9 1.1 constant_dynamic-update-slice_fusion
  445.0 2.4 fusion.45
  447.4 10.5 %fusion.47 = f32[256,1024]{1,0:T(8,128)} fusion(f32[2048,256]{1,0:T(8,128)S(1)} %copy-done.4, f32[2048,1024]{1,0:T(8,128)} %param.11), kind=kOutput, calls=%fused_computation.64 | convolution fusion | flops 6442450944 | bytes 11534336 | tf_op jit(solution)/shard_map/dot_general | solution.py:12
  457.9 37.5 %all-reduce.11.cloned.1.call-done = f32[2048,128]{1,0:T(8,128)} async-done(((f32[2048,128]{1,0:T(8,128)}), f32[2048,128]{1,0:T(8,128)}) %all-reduce.11.cloned.1.call-update) | async-done | bytes 1048592 | tf_op jit(solution)/shard_map/psum | solution.py:23
  495.5 3.7 convolution_bitcast_fusion.1
  499.1 0.0 all-reduce.13.cloned.1.call-update
  499.2 0.0 all-gather.13.cloned.1.call-start
  499.2 57.1 %fusion.44 = f32[4096,128]{1,0:T(8,128)} fusion(f32[2048,4096]{1,0:T(8,128)} %convolution_add_fusion.1, f32[2048,128]{1,0:T(8,128)S(1)} %copy-done.1), kind=kOutput, calls=%fused_computation.61 | convolution fusion | flops 12884901888 | bytes 36700160 | tf_op jit(solution)/shard_map/dot_general | solution.py:12
  556.3 0.0 copy-start.10
  556.3 0.0 all-gather.13.cloned.1.call-update
  556.4 1.2 copy-done.8
  557.5 1.0 fusion.41
  558.5 0.0 all-reduce.13.cloned.1.call-done
  558.5 1.0 fusion.42
  559.6 0.3 fusion.43
  559.9 1.1 fusion.46
  561.0 0.3 convolution_negate_fusion
  561.3 2.2 fusion.24
  563.6 1.0 fusion.10
  564.6 1.0 copy-done.5
  565.5 11.4 %convolution_subtract_fusion = f32[2048,1024]{1,0:T(8,128)} fusion(f32[2048,1024]{1,0:T(8,128)} %param.11, f32[2048,256]{1,0:T(8,128)S(1)} %copy-done.5, f32[256,1024]{1,0:T(8,128)S(1)} %fusion.24), kind=kOutput, calls=%fused_computation.6 | convolution fusion | flops 6444548096 | bytes 19922944 | tf_op jit(solution)/shard_map/dot_general | solution.py:8
  576.9 70.3 %all-gather.13.cloned.1.call-done = f32[32768,128]{1,0:T(8,128)} async-done(((f32[4096,128]{1,0:T(8,128)}), f32[32768,128]{1,0:T(8,128)}) %all-gather.13.cloned.1.call-update) | async-done | bytes 16777232 | tf_op jit(solution)/shard_map/all_gather | solution.py:25
  647.2 8.1 %reduce_sum.19 = f32[4096,128]{1,0:T(8,128)} reduce(f32[8,4096,128]{2,1,0:T(8,128)} %bitcast.65, f32[]{:T(128)} %constant.3.clone.1), dimensions={0}, to_apply=%region_5.0 | reduce | flops 3670016 | bytes 18874372 | tf_op jit(solution)/shard_map/reduce_sum | solution.py:25
  655.3 3.6 fusion.20
  658.9 1.9 fusion
  660.8 33.3 %convolution_add_fusion = f32[2048,4096]{1,0:T(8,128)} fusion(f32[2048,4096]{1,0:T(8,128)} %convolution_add_fusion.1, f32[4096,128]{1,0:T(8,128)S(1)} %copy-done.3, f32[4096,128]{1,0:T(8,128)S(1)} %fusion, f32[2048,128]{1,0:T(8,128)S(1)} %fusion.10, f32[2048,128]{1,0:T(8,128)S(1)} %copy-done.1), kind=kOutput, calls=%fused_computation | convolution fusion | flops 25779765248 | bytes 73400320 | tf_op jit(solution)/shard_map/dot_general | solution.py:33
  (14 shorter events, 0.0 us)
Async XLA Ops:
  7.2 59.7 %all-gather.7.cloned.1.call-start = ((), (), s32[]{:S(2)}) async-start(), calls=%async_computation | async-start | bytes 9437184 | tf_op jit(solution)/shard_map/all_gather | solution.py:61
  7.9 154.6 %all-reduce.7.cloned.1.call-start = ((), (), s32[]{:S(2)}) async-start(), calls=%async_computation.1 | async-start | bytes 2097152 | tf_op jit(solution)/shard_map/psum | solution.py:23
  110.4 52.1 %copy-start = (f32[2048,128]{1,0:T(8,128)S(1)}, f32[2048,128]{1,0:T(8,128)}, u32[]{:S(2)}) copy-start(f32[2048,128]{1,0:T(8,128)} %param.7) | copy-start | bytes 3145732
  110.4 113.1 %all-gather.9.cloned.1.call-start = ((), (), s32[]{:S(2)}) async-start(), calls=%async_computation.3 | async-start | bytes 9437184 | tf_op jit(solution)/shard_map/all_gather | solution.py:62
  111.2 162.9 %all-reduce.9.cloned.1.call-start = ((), (), s32[]{:S(2)}) async-start(), calls=%async_computation.2 | async-start | bytes 131072 | tf_op jit(solution)/shard_map/psum | solution.py:27
  165.5 200.1 %all-gather.11.cloned.1.call-start = ((), (), s32[]{:S(2)}) async-start(), calls=%async_computation.5 | async-start | bytes 18874368 | tf_op jit(solution)/shard_map/all_gather | solution.py:25
  222.4 273.0 %all-reduce.11.cloned.1.call-start = ((), (), s32[]{:S(2)}) async-start(), calls=%async_computation.4 | async-start | bytes 2097152 | tf_op jit(solution)/shard_map/psum | solution.py:23
  223.6 3.2 copy-start.9
  223.6 3.2 copy-start.7
  377.1 1.9 copy-start.6
  379.0 33.4 %copy-start.2 = (f32[4096,128]{1,0:T(8,128)S(1)}, f32[4096,128]{1,0:T(8,128)}, u32[]{:S(2)}) copy-start(f32[4096,128]{1,0:T(8,128)} %constant_dynamic-slice_fusion) | copy-start | bytes 6291460
  412.4 31.4 %copy-start.1 = (f32[2048,128]{1,0:T(8,128)S(1)}, f32[2048,128]{1,0:T(8,128)}, u32[]{:S(2)}) copy-start(f32[2048,128]{1,0:T(8,128)} %param.9) | copy-start | bytes 3145732
  443.4 115.1 %all-reduce.13.cloned.1.call-start = ((), (), s32[]{:S(2)}) async-start(), calls=%async_computation.7 | async-start | bytes 2359296 | tf_op jit(solution)/shard_map/psum | solution.py:27
  445.0 2.4 copy-start.4
  499.2 148.0 %all-gather.13.cloned.1.call-start = ((), (), s32[]{:S(2)}) async-start(), calls=%async_computation.6 | async-start | bytes 18874368 | tf_op jit(solution)/shard_map/all_gather | solution.py:25
  556.3 1.2 copy-start.8
  556.3 1.2 copy-start.10
  563.6 1.9 copy-start.5
  655.3 3.6 copy-start.3
Sparse Core Ops, SparseCore 0:
  9.9 56.9 all-gather.6
  110.6 51.8 all-reduce.6
  164.4 53.5 all-gather.8
  220.8 53.1 all-reduce.8
  276.4 89.1 all-gather.10
  443.5 51.8 all-reduce.10
  499.5 56.7 all-reduce.12
  558.2 88.9 all-gather.12
